TPU v7x, 32 devices: a whole 2x2x4 slice. The times are simulated.
32 devices in a mesh: clip: 2 (over y), tile: 4 (over z), slab: 2 (over x), chan: 2 (over core).
Axes of the slice: x: 2, y: 2, z: 4, core: 2. Of those that a mesh axis runs over, the one named last changes fastest.
Arguments:
- video: bfloat16 [16, 16, 128, 128], P(('clip', 'slab'), 'tile'), parts along dimension 0, may hold values from -6 to 6
- first_weight: bfloat16 [3, 3, 3, 128, 128], P(None, None, None, None, 'chan'), may hold values from -0.109375 to 0.109375
- first_bias: float32 [128], P('chan'), may hold values from -3 to 3
- second_weight: bfloat16 [3, 3, 3, 128, 256], replicated, may hold values from -0.109375 to 0.109375
- second_bias: float32 [256], P('chan'), may hold values from -3 to 3
Outputs:
- latents: bfloat16 [8, 16, 128, 256], P(('clip', 'slab'), 'tile', None, 'chan'), parts along dimension 0
There are 2 independent parts, one for each index of `clip`. A program takes and returns all parts, laid end to end along the dimension named above; an argument that names none is the same for every part. Nothing has to cross between parts.
All inputs are finite; a program needn't handle non-finite values.
Results may differ from a plain program's by a relative error of at most 0.0095.
Values may be sent and summed in bfloat16 or wider, within the bound.
A program may use at most 64 MiB of HBM per device.

v0:
```python
import functools

import jax
import jax.numpy as jnp
from jax import lax
from jax.experimental import pallas as pl
from jax.experimental.pallas import tpu as pltpu
from jax.sharding import PartitionSpec as P

MESH = pl.DeviceIdType.MESH
BACK = 3


def kernel(
    tiles, slabs, video, w1, b1, w2, b2, out,
    v, h, k1, k2, b1_peer, b2_peer, going,
    local_sem, w1_sem, w2_sem, h_send, h_recv, small_send, small_recv, own_send, own_recv,
    x_send, x_recv, z_send, z_recv, p_send, p_recv, o_send, o_recv,
):
    frames, rows, columns, channels = video.shape
    half = rows // 2
    core = lax.axis_index("chan")
    tile = lax.axis_index("tile")
    slab = lax.axis_index("slab")
    other = 1 - core
    z_tile = tile + 2 * core - 1
    has_z = jnp.logical_and(z_tile >= 0, z_tile < tiles)
    no_z = jnp.logical_or(z_tile < 0, z_tile >= tiles)
    has_next = slab < slabs - 1
    has_prev = slab > 0
    peer = {"chan": other}
    z_peer = {"chan": other, "tile": z_tile}
    following = {"slab": slab + 1}
    preceding = {"slab": slab - 1}

    def remote(src, dst, send, recv, device):
        return pltpu.make_async_remote_copy(
            src_ref=src, dst_ref=dst, send_sem=send, recv_sem=recv,
            device_id=device, device_id_type=MESH,
        )

    mine = pl.ds(half * core, half)
    halo_here = pl.ds(rows * core, half)
    halo_there = pl.ds(rows * other, half)
    inner_here = pl.ds(rows * other, half)
    inner_there = pl.ds(rows * core, half)
    arrived = pl.ds(half, half)

    into_v = pltpu.make_async_copy(
        video.at[pl.ds(0, frames - 1)],
        v.at[pl.ds(BACK, frames - 1), pl.ds(half * other, rows)],
        local_sem,
    )
    into_v.start()
    own_w1 = pltpu.make_async_copy(w1, k1.at[:, :, 0], w1_sem)
    own_w1.start()
    part = channels // 2
    width = b2.shape[1]
    w2_copies = []
    for e in range(3):
        for n in range(2):
            for k in range(2):
                owner_n = core if n == 0 else other
                owner_k = core if k == 0 else other
                w2_copies.append(
                    pltpu.make_async_copy(
                        w2.at[:, e, pl.ds(pl.multiple_of(owner_k * part, part), part),
                              pl.ds(pl.multiple_of(owner_n * width, width), width)],
                        k2.at[:, pl.ds(k * part, part), pl.ds((2 * e + n) * width, width)],
                        w2_sem.at[len(w2_copies)],
                    )
                )
    for copy in w2_copies:
        copy.start()

    barrier = pltpu.get_barrier_semaphore()
    everyone = ((None, peer), (has_z, z_peer), (has_next, following), (has_prev, preceding))

    def when(condition, body):
        if condition is None:
            body()
        else:
            pl.when(condition)(body)

    for condition, device in everyone:
        when(condition, lambda device=device: pl.semaphore_signal(
            barrier, inc=1, device_id=device, device_id_type=MESH))
    met = 1 + sum(jnp.where(condition, 1, 0) for condition, _ in everyone[1:])
    pl.semaphore_wait(barrier, met)

    small = [
        remote(w1, k1.at[:, :, 1], small_send.at[0], small_recv.at[0], peer),
        remote(b1, b1_peer, small_send.at[1], small_recv.at[1], peer),
        remote(b2, b2_peer, small_send.at[2], small_recv.at[2], peer),
    ]
    to_next = [
        remote(video.at[frames - BACK + f, mine], v.at[f, arrived], x_send.at[f], x_recv.at[f], following)
        for f in range(BACK)
    ]
    own_z = remote(
        video.at[pl.ds(0, frames - 1), mine],
        v.at[pl.ds(BACK, frames - 1), halo_there],
        own_send, own_recv, z_peer,
    )
    forward_z = [
        remote(v.at[f, arrived], v.at[f, halo_there], z_send.at[f], z_recv.at[f], z_peer)
        for f in range(BACK)
    ]
    forward_p = [
        remote(v.at[f, arrived], v.at[f, inner_there], p_send.at[f], p_recv.at[f], peer)
        for f in range(BACK)
    ]

    small[0].start()

    @pl.when(has_next)
    def _():
        for f in reversed(range(BACK)):
            to_next[f].start()

    @pl.when(has_z)
    def _():
        own_z.start()

    small[1].start()
    small[2].start()

    @pl.when(no_z)
    def _():
        v[:, halo_here] = jnp.zeros((v.shape[0], half, columns, channels), v.dtype)

    @pl.when(slab == 0)
    def _():
        v[0:BACK] = jnp.zeros((BACK,) + v.shape[1:], v.dtype)
        h[0:2] = jnp.zeros((2,) + h.shape[1:], h.dtype)

    def pass_on(f):
        @pl.when(has_prev)
        def _():
            remote(v.at[f, arrived], v.at[f, arrived], x_send.at[f], x_recv.at[f], preceding).wait_recv()
            forward_p[f].start()

            @pl.when(has_z)
            def _():
                forward_z[f].start()

    def ready(f):
        @pl.when(has_prev)
        def _():
            remote(v.at[f, arrived], v.at[f, inner_here], p_send.at[f], p_recv.at[f], peer).wait_recv()

            @pl.when(has_z)
            def _():
                remote(v.at[f, arrived], v.at[f, halo_here], z_send.at[f], z_recv.at[f], z_peer).wait_recv()

    def taps(source, first, count):
        return jnp.concatenate(
            [
                source[first + a, b : b + count].reshape(count * columns, channels)
                for a in range(3)
                for b in range(3)
            ],
            axis=1,
        )

    def shifted_sum(parts, width, bias):
        size = parts.shape[0]
        column = lax.broadcasted_iota(jnp.int32, (size, width), 0) % columns
        before = pltpu.roll(parts[:, 0:width], 1, 0)
        after = pltpu.roll(parts[:, 2 * width : 3 * width], size - 1, 0)
        total = parts[:, width : 2 * width] + jnp.where(column == 0, 0.0, before)
        total = total + jnp.where(column == columns - 1, 0.0, after) + bias
        return total / (1.0 + jnp.exp(-total))

    def hidden(index):
        count = h.shape[1]
        parts = lax.dot_general(
            taps(v, index - 1, count),
            jnp.concatenate([k1[tap].reshape(3 * channels, channels) for tap in range(9)], axis=1),
            (((1,), (1,)), ((), ())),
            preferred_element_type=jnp.float32,
        )
        bias = jnp.concatenate([b1[...], b1_peer[...]], axis=1)
        value = shifted_sum(parts, channels, bias).astype(h.dtype)
        h[index] = value.reshape(count, columns, channels)

        @pl.when(no_z)
        def _():
            h[index, pl.ds((count - 1) * core, 1)] = jnp.zeros((1, columns, channels), h.dtype)

    to_peer = [
        remote(going.at[t], out.at[t, mine], o_send.at[t], o_recv.at[t], peer)
        for t in range(frames // 2)
    ]

    def latent(t):
        parts = jnp.dot(
            taps(h, 2 * t, half), k2[...].reshape(9 * channels, 6 * width),
            preferred_element_type=jnp.float32,
        )
        bias = jnp.concatenate([b2[...], b2_peer[...]], axis=1)
        value = shifted_sum(parts, 2 * width, bias).astype(out.dtype)
        going[t] = value[:, width:].reshape(half, columns, width)
        to_peer[t].start()
        out[t, mine] = value[:, :width].reshape(half, columns, width)

    small[0].wait_recv()
    own_w1.wait()
    small[1].wait_recv()
    small[2].wait_recv()
    pass_on(2)
    into_v.wait()

    @pl.when(has_z)
    def _():
        remote(
            v.at[pl.ds(BACK, frames - 1), halo_here], v.at[pl.ds(BACK, frames - 1), halo_here],
            own_send, own_recv, z_peer,
        ).wait_recv()

    handed = remote(h.at[frames], h.at[0], h_send, h_recv, following)
    hidden(frames)

    @pl.when(has_next)
    def _():
        handed.start()

    for index in range(4, frames):
        hidden(index)
    pass_on(1)
    ready(2)
    hidden(3)
    pass_on(0)
    ready(1)
    hidden(2)
    for copy in w2_copies:
        copy.wait()
    for t in range(1, frames // 2):
        latent(t)
    ready(0)

    @pl.when(has_prev)
    def _():
        hidden(1)
        remote(h.at[0], h.at[0], h_send, h_recv, preceding).wait_recv()

    latent(0)

    for copy in small:
        copy.wait_send()

    @pl.when(has_next)
    def _():
        for copy in to_next:
            copy.wait_send()
        handed.wait_send()

    @pl.when(has_z)
    def _():
        own_z.wait_send()

    @pl.when(has_prev)
    def _():
        for copy in forward_p:
            copy.wait_send()

        @pl.when(has_z)
        def _():
            for copy in forward_z:
                copy.wait_send()

    theirs = pl.ds(half * other, half)
    for t in range(frames // 2):
        remote(going.at[t], out.at[t, theirs], o_send.at[t], o_recv.at[t], peer).wait_recv()
        to_peer[t].wait_send()


def shards(tiles, slabs, video, first_weight, first_bias, second_weight, second_bias):
    frames, rows, columns, channels = video.shape
    half = rows // 2
    assert half == 2 and frames >= 4 and frames % 2 == 0
    part = first_bias.shape[0]
    width = second_bias.shape[0]
    anywhere = pl.BlockSpec(memory_space=pltpu.HBM)
    inside = pl.BlockSpec(memory_space=pltpu.VMEM)
    dma = pltpu.SemaphoreType.DMA
    return pl.pallas_call(
        functools.partial(kernel, tiles, slabs),
        out_shape=jax.ShapeDtypeStruct((frames // 2, rows, columns, width), jnp.bfloat16),
        in_specs=[anywhere, anywhere, inside, anywhere, inside],
        out_specs=inside,
        scratch_shapes=[
            pltpu.VMEM((BACK + frames - 1, rows + 2, columns, channels), jnp.bfloat16),
            pltpu.VMEM((frames + 1, half + 2, columns, channels), jnp.bfloat16),
            pltpu.VMEM((9, 3, 2, part, channels), jnp.bfloat16),
            pltpu.VMEM((9, channels, 6 * width), jnp.bfloat16),
            pltpu.VMEM((1, part), jnp.float32),
            pltpu.VMEM((1, width), jnp.float32),
            pltpu.VMEM((frames // 2, half, columns, width), jnp.bfloat16),
            dma, dma, dma((12,)), dma, dma, dma((3,)), dma((3,)), dma, dma,
            dma((BACK,)), dma((BACK,)), dma((BACK,)), dma((BACK,)), dma((BACK,)), dma((BACK,)),
            dma((frames // 2,)), dma((frames // 2,)),
        ],
        compiler_params=pltpu.CompilerParams(
            collective_id=0, has_side_effects=True, vmem_limit_bytes=58000 << 10
        ),
    )(
        video,
        jnp.swapaxes(first_weight, 3, 4).reshape(9, 3, part, channels),
        first_bias.reshape(1, part),
        second_weight.reshape(9, 3, channels, 2 * width),
        second_bias.reshape(1, width),
    )


def solution(mesh):
    placed = (
        P(("clip", "slab"), "tile", None, None),
        P(None, None, None, None, "chan"),
        P("chan"),
        P(),
        P("chan"),
    )
    return jax.shard_map(
        functools.partial(shards, mesh.shape["tile"], mesh.shape["slab"]),
        mesh=mesh,
        in_specs=placed,
        out_specs=P(("clip", "slab"), "tile", None, "chan"),
        check_vma=False,
    )
```

profile of v0, /device:TPU:11, one launch (start us, length us, event | category | flops | bytes accessed | tf_op | source)
XLA Modules:
  0.0 18.5 jit_solution(11940612763400786609)
XLA Ops:
  0.0 16.8 %shard_map.55 = bf16[2,4,128,128]{3,2,1,0:T(8,128)(2,1)} custom-call(bf16[4,4,128,128]{3,2,1,0:T(8,128)(2,1)} %video.1, bf16[9,3,64,128]{3,2,1,0:T(8,128)(2,1)} %bitcast.7, f32[1,64]{1,0:T(1,128)} %bitcast.8, bf16[9,3,128,256]{3,2,1,0:T(8,128)(2,1)} %bitcast.6, f32[1,128]{1,0:T(1,128)} %bitcast.9), custom_call_target="tpu_custom_call" | custom-call | tf_op jit(solution)/shard_map/pallas_call | solution.py:287
  16.8 1.7 %copy.7 = bf16[2,4,128,128]{3,2,1,0:T(8,128)(2,1)} copy(bf16[2,4,128,128]{3,2,1,0:T(8,128)(2,1)} %shard_map.55) | data formatting | bytes 524288
where the time goes:
time: 18.7 us; the launch traced here: 18.5 us
  Pallas kernels  16.8 us (90%)
  local copies, waits for them, and re-layouts  1.67 us (9%)
    pallas_call x1, Pallas kernels, shards(): pl.pallas_call(functools.partial(kernel, tiles, slabs), out_shape=jax.Sha...  16.8 us
    unnamed x1, local copies, waits for them, and re-layouts  1.67 us

commit v1 on v0

--- a/solution.py
+++ b/solution.py
@@ -144,19 +144,20 @@
             def _():
                 forward_z[f].start()
 
-    def ready(f):
+    def inner_ready(f):
         @pl.when(has_prev)
         def _():
             remote(v.at[f, arrived], v.at[f, inner_here], p_send.at[f], p_recv.at[f], peer).wait_recv()
 
-            @pl.when(has_z)
-            def _():
-                remote(v.at[f, arrived], v.at[f, halo_here], z_send.at[f], z_recv.at[f], z_peer).wait_recv()
-
-    def taps(source, first, count):
+    def outer_ready(f):
+        @pl.when(jnp.logical_and(has_prev, has_z))
+        def _():
+            remote(v.at[f, arrived], v.at[f, halo_here], z_send.at[f], z_recv.at[f], z_peer).wait_recv()
+
+    def taps(source, index, first, count):
         return jnp.concatenate(
             [
-                source[first + a, b : b + count].reshape(count * columns, channels)
+                source[index + a, pl.ds(first + b, count)].reshape(count * columns, channels)
                 for a in range(3)
                 for b in range(3)
             ],
@@ -172,21 +173,26 @@
         total = total + jnp.where(column == columns - 1, 0.0, after) + bias
         return total / (1.0 + jnp.exp(-total))
 
-    def hidden(index):
-        count = h.shape[1]
+    def hidden_rows(index, first):
         parts = lax.dot_general(
-            taps(v, index - 1, count),
+            taps(v, index - 1, first, half),
             jnp.concatenate([k1[tap].reshape(3 * channels, channels) for tap in range(9)], axis=1),
             (((1,), (1,)), ((), ())),
             preferred_element_type=jnp.float32,
         )
         bias = jnp.concatenate([b1[...], b1_peer[...]], axis=1)
         value = shifted_sum(parts, channels, bias).astype(h.dtype)
-        h[index] = value.reshape(count, columns, channels)
+        h[index, pl.ds(first, half)] = value.reshape(half, columns, channels)
+
+    def inner(index):
+        hidden_rows(index, half * other)
+
+    def outer(index):
+        hidden_rows(index, half * core)
 
         @pl.when(no_z)
         def _():
-            h[index, pl.ds((count - 1) * core, 1)] = jnp.zeros((1, columns, channels), h.dtype)
+            h[index, pl.ds((rows - 1) * core, 1)] = jnp.zeros((1, columns, channels), h.dtype)
 
     to_peer = [
         remote(going.at[t], out.at[t, mine], o_send.at[t], o_recv.at[t], peer)
@@ -195,7 +201,7 @@
 
     def latent(t):
         parts = jnp.dot(
-            taps(h, 2 * t, half), k2[...].reshape(9 * channels, 6 * width),
+            taps(h, 2 * t, 0, half), k2[...].reshape(9 * channels, 6 * width),
             preferred_element_type=jnp.float32,
         )
         bias = jnp.concatenate([b2[...], b2_peer[...]], axis=1)
@@ -208,8 +214,10 @@
     own_w1.wait()
     small[1].wait_recv()
     small[2].wait_recv()
+    into_v.wait()
+    handed = remote(h.at[frames], h.at[0], h_send, h_recv, following)
+    inner(frames)
     pass_on(2)
-    into_v.wait()
 
     @pl.when(has_z)
     def _():
@@ -218,30 +226,36 @@
             own_send, own_recv, z_peer,
         ).wait_recv()
 
-    handed = remote(h.at[frames], h.at[0], h_send, h_recv, following)
-    hidden(frames)
+    outer(frames)
 
     @pl.when(has_next)
     def _():
         handed.start()
 
-    for index in range(4, frames):
-        hidden(index)
     pass_on(1)
-    ready(2)
-    hidden(3)
+    inner_ready(2)
+    for index in range(frames - 1, 3, -1):
+        inner(index)
+        outer(index)
+    inner(3)
     pass_on(0)
-    ready(1)
-    hidden(2)
+    outer_ready(2)
+    outer(3)
+    inner_ready(1)
+    inner(2)
+    outer_ready(1)
+    outer(2)
     for copy in w2_copies:
         copy.wait()
     for t in range(1, frames // 2):
         latent(t)
-    ready(0)
+    inner_ready(0)
 
     @pl.when(has_prev)
     def _():
-        hidden(1)
+        inner(1)
+        outer_ready(0)
+        outer(1)
         remote(h.at[0], h.at[0], h_send, h_recv, preceding).wait_recv()
 
     latent(0)
@@ -302,14 +316,19 @@
             dma((frames // 2,)), dma((frames // 2,)),
         ],
         compiler_params=pltpu.CompilerParams(
-            collective_id=0, has_side_effects=True, vmem_limit_bytes=58000 << 10
+            collective_id=0, has_side_effects=True, vmem_limit_bytes=32 << 20
         ),
     )(
-        video,
-        jnp.swapaxes(first_weight, 3, 4).reshape(9, 3, part, channels),
-        first_bias.reshape(1, part),
-        second_weight.reshape(9, 3, channels, 2 * width),
-        second_bias.reshape(1, width),
+        *(
+            pltpu.with_memory_space_constraint(operand, pltpu.HBM)
+            for operand in (
+                video,
+                jnp.swapaxes(first_weight, 3, 4).reshape(9, 3, part, channels),
+                first_bias.reshape(1, part),
+                second_weight.reshape(9, 3, channels, 2 * width),
+                second_bias.reshape(1, width),
+            )
+        )
     )
 
 

time: 18.7 us -> 16.5 us (0.88)
  Pallas kernels: 16.8 us -> 15.6 us
  local copies, waits for them, and re-layouts: 1.67 us -> 0.71 us
    pallas_call x1, Pallas kernels: 16.8 us -> 15.6 us  [shards(): pl.pallas_call(functools.partial(kernel, tiles, slabs), out_shape=jax.Sha...]
    unnamed x1, local copies, waits for them, and re-layouts: 1.67 us -> 0.71 us
where the time goes in v1:
time: 16.5 us; the launch traced here: 16.4 us
  Pallas kernels  15.6 us (95%)
  local copies, waits for them, and re-layouts  0.71 us (4%)
    pallas_call x1, Pallas kernels, shards(): pl.pallas_call(functools.partial(kernel, tiles, slabs), out_shape=jax.Sha...  15.6 us
    unnamed x1, local copies, waits for them, and re-layouts  0.71 us

profile of v1, /device:TPU:11, one launch (start us, length us, event | category | flops | bytes accessed | tf_op | source)
XLA Modules:
  0.0 16.4 jit_solution(14089673975810884930)
XLA Ops:
  0.0 15.6 %shard_map.55 = bf16[2,4,128,128]{3,2,1,0:T(8,128)(2,1)S(1)} custom-call(bf16[4,4,128,128]{3,2,1,0:T(8,128)(2,1)} %video.1, bf16[9,3,64,128]{3,2,1,0:T(8,128)(2,1)} %bitcast.7, f32[1,64]{1,0:T(1,128)} %bitcast.8, bf16[9,3,128,256]{3,2,1,0:T(8,128)(2,1)} %bitcast.6, f32[1,128]{1,0:T(1,128)} %bitcast.9), custom_call_target="tpu_custom_call" | custom-call | tf_op jit(solution)/shard_map/pallas_call | solution.py:301
  15.7 0.7 %copy.7 = bf16[2,4,128,128]{3,2,1,0:T(8,128)(2,1)} copy(bf16[2,4,128,128]{3,2,1,0:T(8,128)(2,1)S(1)} %shard_map.55) | data formatting | bytes 524288

commit v2 on v1

--- a/solution.py
+++ b/solution.py
@@ -47,8 +47,8 @@
     arrived = pl.ds(half, half)
 
     into_v = pltpu.make_async_copy(
-        video.at[pl.ds(0, frames - 1)],
-        v.at[pl.ds(BACK, frames - 1), pl.ds(half * other, rows)],
+        video,
+        v.at[pl.ds(BACK, frames), pl.ds(half * other, rows)],
         local_sem,
     )
     into_v.start()
@@ -70,9 +70,6 @@
                         w2_sem.at[len(w2_copies)],
                     )
                 )
-    for copy in w2_copies:
-        copy.start()
-
     barrier = pltpu.get_barrier_semaphore()
     everyone = ((None, peer), (has_z, z_peer), (has_next, following), (has_prev, preceding))
 
@@ -85,20 +82,22 @@
     for condition, device in everyone:
         when(condition, lambda device=device: pl.semaphore_signal(
             barrier, inc=1, device_id=device, device_id_type=MESH))
+    into_v.wait()
+    own_w1.wait()
     met = 1 + sum(jnp.where(condition, 1, 0) for condition, _ in everyone[1:])
     pl.semaphore_wait(barrier, met)
 
     small = [
-        remote(w1, k1.at[:, :, 1], small_send.at[0], small_recv.at[0], peer),
+        remote(k1.at[:, :, 0], k1.at[:, :, 1], small_send.at[0], small_recv.at[0], peer),
         remote(b1, b1_peer, small_send.at[1], small_recv.at[1], peer),
         remote(b2, b2_peer, small_send.at[2], small_recv.at[2], peer),
     ]
     to_next = [
-        remote(video.at[frames - BACK + f, mine], v.at[f, arrived], x_send.at[f], x_recv.at[f], following)
+        remote(v.at[frames + f, arrived], v.at[f, arrived], x_send.at[f], x_recv.at[f], following)
         for f in range(BACK)
     ]
     own_z = remote(
-        video.at[pl.ds(0, frames - 1), mine],
+        v.at[pl.ds(BACK, frames - 1), arrived],
         v.at[pl.ds(BACK, frames - 1), halo_there],
         own_send, own_recv, z_peer,
     )
@@ -124,6 +123,8 @@
 
     small[1].start()
     small[2].start()
+    for copy in w2_copies:
+        copy.start()
 
     @pl.when(no_z)
     def _():
@@ -173,23 +174,29 @@
         total = total + jnp.where(column == columns - 1, 0.0, after) + bias
         return total / (1.0 + jnp.exp(-total))
 
-    def hidden_rows(index, first):
+    def hidden_rows(index, first, count):
         parts = lax.dot_general(
-            taps(v, index - 1, first, half),
+            taps(v, index - 1, first, count),
             jnp.concatenate([k1[tap].reshape(3 * channels, channels) for tap in range(9)], axis=1),
             (((1,), (1,)), ((), ())),
             preferred_element_type=jnp.float32,
         )
         bias = jnp.concatenate([b1[...], b1_peer[...]], axis=1)
         value = shifted_sum(parts, channels, bias).astype(h.dtype)
-        h[index, pl.ds(first, half)] = value.reshape(half, columns, channels)
+        h[index, pl.ds(first, count)] = value.reshape(count, columns, channels)
 
     def inner(index):
-        hidden_rows(index, half * other)
+        hidden_rows(index, half * other, half)
 
     def outer(index):
-        hidden_rows(index, half * core)
-
+        hidden_rows(index, half * core, half)
+        clear_outside(index)
+
+    def whole(index):
+        hidden_rows(index, 0, rows)
+        clear_outside(index)
+
+    def clear_outside(index):
         @pl.when(no_z)
         def _():
             h[index, pl.ds((rows - 1) * core, 1)] = jnp.zeros((1, columns, channels), h.dtype)
@@ -204,17 +211,24 @@
             taps(h, 2 * t, 0, half), k2[...].reshape(9 * channels, 6 * width),
             preferred_element_type=jnp.float32,
         )
-        bias = jnp.concatenate([b2[...], b2_peer[...]], axis=1)
-        value = shifted_sum(parts, 2 * width, bias).astype(out.dtype)
-        going[t] = value[:, width:].reshape(half, columns, width)
-        to_peer[t].start()
-        out[t, mine] = value[:, :width].reshape(half, columns, width)
+        for start, bias in ((width, b2_peer[...]), (0, b2[...])):
+            chosen = jnp.concatenate(
+                [
+                    parts[:, 2 * width * e + start : 2 * width * e + start + width]
+                    for e in range(3)
+                ],
+                axis=1,
+            )
+            value = shifted_sum(chosen, width, bias).astype(out.dtype).reshape(half, columns, width)
+            if start:
+                going[t] = value
+                to_peer[t].start()
+            else:
+                out[t, mine] = value
 
     small[0].wait_recv()
-    own_w1.wait()
     small[1].wait_recv()
     small[2].wait_recv()
-    into_v.wait()
     handed = remote(h.at[frames], h.at[0], h_send, h_recv, following)
     inner(frames)
     pass_on(2)
@@ -253,9 +267,8 @@
 
     @pl.when(has_prev)
     def _():
-        inner(1)
         outer_ready(0)
-        outer(1)
+        whole(1)
         remote(h.at[0], h.at[0], h_send, h_recv, preceding).wait_recv()
 
     latent(0)
@@ -304,7 +317,7 @@
         in_specs=[anywhere, anywhere, inside, anywhere, inside],
         out_specs=inside,
         scratch_shapes=[
-            pltpu.VMEM((BACK + frames - 1, rows + 2, columns, channels), jnp.bfloat16),
+            pltpu.VMEM((BACK + frames, rows + 2, columns, channels), jnp.bfloat16),
             pltpu.VMEM((frames + 1, half + 2, columns, channels), jnp.bfloat16),
             pltpu.VMEM((9, 3, 2, part, channels), jnp.bfloat16),
             pltpu.VMEM((9, channels, 6 * width), jnp.bfloat16),

time: 16.5 us -> 16.1 us (0.976)
  Pallas kernels: 15.6 us -> 15.2 us
    pallas_call x1, Pallas kernels: 15.6 us -> 15.2 us  [shards(): pl.pallas_call(functools.partial(kernel, tiles, slabs), out_shape=jax.Sha...]
where the time goes in v2:
time: 16.1 us; the launch traced here: 15.9 us
  Pallas kernels  15.2 us (94%)
  local copies, waits for them, and re-layouts  0.71 us (4%)
    pallas_call x1, Pallas kernels, shards(): pl.pallas_call(functools.partial(kernel, tiles, slabs), out_shape=jax.Sha...  15.2 us
    unnamed x1, local copies, waits for them, and re-layouts  0.71 us

profile of v2, /device:TPU:11, one launch (start us, length us, event | category | flops | bytes accessed | tf_op | source)
XLA Modules:
  0.0 15.9 jit_solution(4708780845406263216)
XLA Ops:
  0.0 15.2 %shard_map.55 = bf16[2,4,128,128]{3,2,1,0:T(8,128)(2,1)S(1)} custom-call(bf16[4,4,128,128]{3,2,1,0:T(8,128)(2,1)} %video.1, bf16[9,3,64,128]{3,2,1,0:T(8,128)(2,1)} %bitcast.7, f32[1,64]{1,0:T(1,128)} %bitcast.8, bf16[9,3,128,256]{3,2,1,0:T(8,128)(2,1)} %bitcast.6, f32[1,128]{1,0:T(1,128)} %bitcast.9), custom_call_target="tpu_custom_call" | custom-call | tf_op jit(solution)/shard_map/pallas_call | solution.py:314
  15.2 0.7 %copy.7 = bf16[2,4,128,128]{3,2,1,0:T(8,128)(2,1)} copy(bf16[2,4,128,128]{3,2,1,0:T(8,128)(2,1)S(1)} %shard_map.55) | data formatting | bytes 524288

commit v3 on v2

--- a/solution.py
+++ b/solution.py
@@ -8,13 +8,13 @@
 from jax.sharding import PartitionSpec as P
 
 MESH = pl.DeviceIdType.MESH
-BACK = 3
+BACK = 2
 
 
 def kernel(
     tiles, slabs, video, w1, b1, w2, b2, out,
     v, h, k1, k2, b1_peer, b2_peer, going,
-    local_sem, w1_sem, w2_sem, h_send, h_recv, small_send, small_recv, own_send, own_recv,
+    local_sem, w1_sem, w2_sem, h_send, h_recv, e_send, e_recv, q_send, q_recv, small_send, small_recv, own_send, own_recv,
     x_send, x_recv, z_send, z_recv, p_send, p_recv, o_send, o_recv,
 ):
     frames, rows, columns, channels = video.shape
@@ -97,8 +97,8 @@
         for f in range(BACK)
     ]
     own_z = remote(
-        v.at[pl.ds(BACK, frames - 1), arrived],
-        v.at[pl.ds(BACK, frames - 1), halo_there],
+        v.at[pl.ds(BACK, frames), arrived],
+        v.at[pl.ds(BACK, frames), halo_there],
         own_send, own_recv, z_peer,
     )
     forward_z = [
@@ -130,11 +130,6 @@
     def _():
         v[:, halo_here] = jnp.zeros((v.shape[0], half, columns, channels), v.dtype)
 
-    @pl.when(slab == 0)
-    def _():
-        v[0:BACK] = jnp.zeros((BACK,) + v.shape[1:], v.dtype)
-        h[0:2] = jnp.zeros((2,) + h.shape[1:], h.dtype)
-
     def pass_on(f):
         @pl.when(has_prev)
         def _():
@@ -155,11 +150,11 @@
         def _():
             remote(v.at[f, arrived], v.at[f, halo_here], z_send.at[f], z_recv.at[f], z_peer).wait_recv()
 
-    def taps(source, index, first, count):
+    def taps(source, index, first, count, oldest=0):
         return jnp.concatenate(
             [
                 source[index + a, pl.ds(first + b, count)].reshape(count * columns, channels)
-                for a in range(3)
+                for a in range(oldest, 3)
                 for b in range(3)
             ],
             axis=1,
@@ -174,10 +169,10 @@
         total = total + jnp.where(column == columns - 1, 0.0, after) + bias
         return total / (1.0 + jnp.exp(-total))
 
-    def hidden_rows(index, first, count):
+    def hidden_rows(index, first, count, oldest=0):
         parts = lax.dot_general(
-            taps(v, index - 1, first, count),
-            jnp.concatenate([k1[tap].reshape(3 * channels, channels) for tap in range(9)], axis=1),
+            taps(v, index - 2, first, count, oldest),
+            jnp.concatenate([k1[tap].reshape(3 * channels, channels) for tap in range(3 * oldest, 9)], axis=1),
             (((1,), (1,)), ((), ())),
             preferred_element_type=jnp.float32,
         )
@@ -192,8 +187,8 @@
         hidden_rows(index, half * core, half)
         clear_outside(index)
 
-    def whole(index):
-        hidden_rows(index, 0, rows)
+    def whole(index, oldest=0):
+        hidden_rows(index, 0, rows, oldest)
         clear_outside(index)
 
     def clear_outside(index):
@@ -206,9 +201,10 @@
         for t in range(frames // 2)
     ]
 
-    def latent(t):
+    def latent(t, oldest=0):
         parts = jnp.dot(
-            taps(h, 2 * t, 0, half), k2[...].reshape(9 * channels, 6 * width),
+            taps(h, 2 * t, 0, half, oldest),
+            k2[3 * oldest :].reshape((9 - 3 * oldest) * channels, 6 * width),
             preferred_element_type=jnp.float32,
         )
         for start, bias in ((width, b2_peer[...]), (0, b2[...])):
@@ -229,14 +225,37 @@
     small[0].wait_recv()
     small[1].wait_recv()
     small[2].wait_recv()
-    handed = remote(h.at[frames], h.at[0], h_send, h_recv, following)
+    early = pl.ds(2 - core, 1)
+    early_there = pl.ds((rows - 1) * core, 1)
+    early_here = pl.ds((rows - 1) * other, 1)
+    late = pl.ds(half * core, half)
+    hand_early = [
+        remote(h.at[frames + f, early], h.at[f, early], e_send.at[f], e_recv.at[f], following)
+        for f in range(2)
+    ]
+    hand_late = [
+        remote(h.at[frames + f, late], h.at[f, late], h_send.at[f], h_recv.at[f], following)
+        for f in range(2)
+    ]
+    share = [
+        remote(h.at[f, early], h.at[f, early_there], q_send.at[f], q_recv.at[f], peer)
+        for f in range(2)
+    ]
+
     inner(frames)
-    pass_on(2)
+
+    @pl.when(has_next)
+    def _():
+        hand_early[0].start()
+        inner(frames + 1)
+        hand_early[1].start()
+
+    pass_on(1)
 
     @pl.when(has_z)
     def _():
         remote(
-            v.at[pl.ds(BACK, frames - 1), halo_here], v.at[pl.ds(BACK, frames - 1), halo_here],
+            v.at[pl.ds(BACK, frames), halo_here], v.at[pl.ds(BACK, frames), halo_here],
             own_send, own_recv, z_peer,
         ).wait_recv()
 
@@ -244,34 +263,51 @@
 
     @pl.when(has_next)
     def _():
-        handed.start()
-
-    pass_on(1)
-    inner_ready(2)
+        hand_late[0].start()
+        outer(frames + 1)
+        hand_late[1].start()
+
+    pass_on(0)
     for index in range(frames - 1, 3, -1):
-        inner(index)
-        outer(index)
-    inner(3)
-    pass_on(0)
-    outer_ready(2)
-    outer(3)
-    inner_ready(1)
-    inner(2)
-    outer_ready(1)
-    outer(2)
+        whole(index)
+
+    @pl.when(has_prev)
+    def _():
+        inner_ready(1)
+        inner(3)
+        outer_ready(1)
+        outer(3)
+        for f in range(2):
+            remote(h.at[f, early], h.at[f, early], e_send.at[f], e_recv.at[f], preceding).wait_recv()
+            share[f].start()
+        inner_ready(0)
+        inner(2)
+        outer_ready(0)
+        outer(2)
+
+    @pl.when(slab == 0)
+    def _():
+        whole(3, 1)
+        whole(2, 2)
+
     for copy in w2_copies:
         copy.wait()
     for t in range(1, frames // 2):
         latent(t)
-    inner_ready(0)
 
     @pl.when(has_prev)
     def _():
-        outer_ready(0)
-        whole(1)
-        remote(h.at[0], h.at[0], h_send, h_recv, preceding).wait_recv()
-
-    latent(0)
+        for f in range(2):
+            remote(h.at[f, early], h.at[f, early_here], q_send.at[f], q_recv.at[f], peer).wait_recv()
+            remote(h.at[f, late], h.at[f, late], h_send.at[f], h_recv.at[f], preceding).wait_recv()
+            shared = h[f, early_here].reshape(columns, channels)
+            shared = jnp.concatenate([shared[:, part:], shared[:, :part]], axis=1)
+            h[f, early_here] = shared.reshape(1, columns, channels)
+        latent(0)
+
+    @pl.when(slab == 0)
+    def _():
+        latent(0, 2)
 
     for copy in small:
         copy.wait_send()
@@ -280,7 +316,8 @@
     def _():
         for copy in to_next:
             copy.wait_send()
-        handed.wait_send()
+        for copy in hand_early + hand_late:
+            copy.wait_send()
 
     @pl.when(has_z)
     def _():
@@ -288,7 +325,7 @@
 
     @pl.when(has_prev)
     def _():
-        for copy in forward_p:
+        for copy in forward_p + share:
             copy.wait_send()
 
         @pl.when(has_z)
@@ -318,13 +355,13 @@
         out_specs=inside,
         scratch_shapes=[
             pltpu.VMEM((BACK + frames, rows + 2, columns, channels), jnp.bfloat16),
-            pltpu.VMEM((frames + 1, half + 2, columns, channels), jnp.bfloat16),
+            pltpu.VMEM((frames + 2, half + 2, columns, channels), jnp.bfloat16),
             pltpu.VMEM((9, 3, 2, part, channels), jnp.bfloat16),
             pltpu.VMEM((9, channels, 6 * width), jnp.bfloat16),
             pltpu.VMEM((1, part), jnp.float32),
             pltpu.VMEM((1, width), jnp.float32),
             pltpu.VMEM((frames // 2, half, columns, width), jnp.bfloat16),
-            dma, dma, dma((12,)), dma, dma, dma((3,)), dma((3,)), dma, dma,
+            dma, dma, dma((12,)), dma((2,)), dma((2,)), dma((2,)), dma((2,)), dma((2,)), dma((2,)), dma((3,)), dma((3,)), dma, dma,
             dma((BACK,)), dma((BACK,)), dma((BACK,)), dma((BACK,)), dma((BACK,)), dma((BACK,)),
             dma((frames // 2,)), dma((frames // 2,)),
         ],

time: 16.1 us -> 15.5 us (0.963)
  Pallas kernels: 15.2 us -> 14.6 us
    pallas_call x1, Pallas kernels: 15.2 us -> 14.6 us  [shards(): pl.pallas_call(functools.partial(kernel, tiles, slabs), out_shape=jax.Sha...]
where the time goes in v3:
time: 15.5 us; the launch traced here: 15.3 us
  Pallas kernels  14.6 us (94%)
  local copies, waits for them, and re-layouts  0.71 us (5%)
    pallas_call x1, Pallas kernels, shards(): pl.pallas_call(functools.partial(kernel, tiles, slabs), out_shape=jax.Sha...  14.6 us
    unnamed x1, local copies, waits for them, and re-layouts  0.71 us

profile of v3, /device:TPU:11, one launch (start us, length us, event | category | flops | bytes accessed | tf_op | source)
XLA Modules:
  0.0 15.3 jit_solution(512401131084866791)
XLA Ops:
  0.0 14.6 %shard_map.55 = bf16[2,4,128,128]{3,2,1,0:T(8,128)(2,1)S(1)} custom-call(bf16[4,4,128,128]{3,2,1,0:T(8,128)(2,1)} %video.1, bf16[9,3,64,128]{3,2,1,0:T(8,128)(2,1)} %bitcast.7, f32[1,64]{1,0:T(1,128)} %bitcast.8, bf16[9,3,128,256]{3,2,1,0:T(8,128)(2,1)} %bitcast.6, f32[1,128]{1,0:T(1,128)} %bitcast.9), custom_call_target="tpu_custom_call" | custom-call | tf_op jit(solution)/shard_map/pallas_call | solution.py:351
  14.6 0.7 %copy.7 = bf16[2,4,128,128]{3,2,1,0:T(8,128)(2,1)} copy(bf16[2,4,128,128]{3,2,1,0:T(8,128)(2,1)S(1)} %shard_map.55) | data formatting | bytes 524288
